TPU v7x, 32 devices: a whole 2x2x4 slice. The times are simulated.
32 devices in a mesh: dp: 8 (over z, y), seq: 4 (over x, core).
Axes of the slice: x: 2, y: 2, z: 4, core: 2. Of those that a mesh axis runs over, the one named last changes fastest.
Arguments:
- tokens: bfloat16 [8, 512, 1024], P('dp', 'seq'), may hold values from -6 to 6
- cache_keys: bfloat16 [8, 2048, 1024], P('dp', 'seq')
- cache_values: bfloat16 [8, 2048, 1024], P('dp', 'seq'), may hold values from -6 to 6
- qkv_weight: bfloat16 [1024, 3072], P(None, 'seq'), may hold values from -0.1875 to 0.1875
- qkv_bias: float32 [3072], replicated, may hold values from -3 to 3
- out_weight: bfloat16 [1024, 1024], P('seq', 'dp'), may hold values from -0.1875 to 0.1875
- out_bias: float32 [1024], replicated, may hold values from -3 to 3
- norm_gain: float32 [1024], replicated, may hold values from 0.1 to 1.9
- norm_bias: float32 [1024], replicated, may hold values from -3 to 3
- cached_len: int32 [8], replicated, may hold values from 0 to 2048, as said below
- span_len: int32 [8], replicated, may hold values from 1 to 512, as said below
- slot_request: int32 [8], replicated, may hold values from 0 to 7, each once
Outputs:
- normed: bfloat16 [8, 512, 1024], P('dp', 'seq')
Inputs may be any that keep to these rules, and one draw needn't show every extreme that they name: `cached_len`: some request has exactly 2048 cached positions. `span_len`: some request has exactly 512 new tokens in use. `slot_request`: each request names one slot.
All inputs are finite; a program needn't handle non-finite values.
Results may differ from a plain program's by a relative error of at most 0.0085.
Values may be sent and summed in bfloat16 or wider, within the bound.
A program may use at most 64 MiB of HBM per device.

v0:
```python
import jax
import jax.numpy as jnp
from jax import lax
from jax.sharding import PartitionSpec as P

D = 1024
HEADS = 16
HEAD_DIM = 64
neg_big = -1e30


def local(
    tokens,
    cache_keys,
    cache_values,
    qkv_weight,
    qkv_bias,
    out_weight,
    out_bias,
    norm_gain,
    norm_bias,
    cached_len,
    span_len,
    slot_request,
):
    seq_index = lax.axis_index("seq")
    dp_index = lax.axis_index("dp")
    groups = lax.axis_size("seq")
    request = slot_request[dp_index]
    cached = cached_len[request]
    filled = span_len[request]
    inputs = tokens[0]
    own_rows = inputs.shape[0]
    cache_rows = cache_keys.shape[1]
    all_rows = own_rows * groups
    scale = HEAD_DIM ** (-0.5)
    qkv_full = lax.all_gather(qkv_weight, "seq", axis=1, tiled=True)
    summed = jnp.dot(inputs, qkv_full, preferred_element_type=jnp.float32)
    projected = (summed + qkv_bias).astype(jnp.bfloat16)
    split = projected.reshape(own_rows, HEADS, 3, HEAD_DIM)
    own_queries = split[:, :, 0].reshape(own_rows, D)
    new_keys = split[:, :, 1].reshape(own_rows, D)
    new_values = split[:, :, 2].reshape(own_rows, D)
    all_queries = lax.all_gather(own_queries, "seq", axis=0, tiled=True)
    keys = jnp.concatenate([cache_keys[0], new_keys], 0)
    values = jnp.concatenate([cache_values[0], new_values], 0)
    positions = jnp.arange(all_rows)
    cache_pos = seq_index * cache_rows + jnp.arange(cache_rows)
    new_pos = seq_index * own_rows + jnp.arange(own_rows)
    live_cache = jnp.broadcast_to(cache_pos[None, :] < cached, (all_rows, cache_rows))
    live_new = (new_pos[None, :] <= positions[:, None]) & (new_pos[None, :] < filled)
    live = jnp.concatenate([live_cache, live_new], 1)

    def attend(head, carry):
        outputs, tops, totals = carry
        start = head * HEAD_DIM
        query = lax.dynamic_slice_in_dim(all_queries, start, HEAD_DIM, 1)
        key_block = lax.dynamic_slice_in_dim(keys, start, HEAD_DIM, 1)
        value_block = lax.dynamic_slice_in_dim(values, start, HEAD_DIM, 1)
        scores = (
            lax.dot_general(
                query, key_block, (((1,), (1,)), ((), ())), preferred_element_type=jnp.float32
            )
            * scale
        )
        masked = jnp.where(live, scores, neg_big)
        top = jnp.max(masked, axis=1)
        weights = jnp.where(live, jnp.exp(masked - top[:, None]), 0.0)
        total = jnp.sum(weights, axis=1)
        numer = jnp.dot(
            weights.astype(jnp.bfloat16), value_block, preferred_element_type=jnp.float32
        )
        result = (numer / jnp.maximum(total, 1.0)[:, None]).astype(jnp.bfloat16)
        outputs = lax.dynamic_update_slice_in_dim(outputs, result, start, 1)
        tops = lax.dynamic_update_slice(tops, top[:, None], (0, head))
        totals = lax.dynamic_update_slice(totals, total[:, None], (0, head))
        return (outputs, tops, totals)

    start_state = (
        jnp.zeros((all_rows, D), jnp.bfloat16),
        jnp.zeros((all_rows, HEADS), jnp.float32),
        jnp.zeros((all_rows, HEADS), jnp.float32),
    )
    partial_value, tops, totals = lax.fori_loop(0, HEADS, attend, start_state)
    partial_wide = partial_value.astype(jnp.float32)
    every_partial, every_top, every_total = (
        lax.all_gather(partial_wide[None], "seq", axis=0, tiled=True),
        lax.all_gather(tops[None], "seq", axis=0, tiled=True),
        lax.all_gather(totals[None], "seq", axis=0, tiled=True),
    )
    mine_partial = lax.dynamic_slice_in_dim(every_partial, seq_index * own_rows, own_rows, 1)
    mine_top = lax.dynamic_slice_in_dim(every_top, seq_index * own_rows, own_rows, 1)
    mine_total = lax.dynamic_slice_in_dim(every_total, seq_index * own_rows, own_rows, 1)
    best = jnp.max(mine_top, axis=0)
    share = mine_total * jnp.exp(mine_top - best[None])
    denom = jnp.sum(share, axis=0)
    spread_parts = mine_partial.reshape(groups, own_rows, HEADS, HEAD_DIM)
    attn = (
        (jnp.sum(share[:, :, :, None] * spread_parts, axis=0) / denom[:, :, None])
        .reshape(own_rows, D)
        .astype(jnp.bfloat16)
    )
    head_rows = lax.all_gather(out_weight, "dp", axis=1, tiled=True)
    out_full = lax.all_gather(head_rows, "seq", axis=0, tiled=True)
    projected_out = jnp.dot(attn, out_full, preferred_element_type=jnp.float32)
    mixed = projected_out + out_bias + inputs.astype(jnp.float32)
    center = mixed - jnp.mean(mixed, axis=1, keepdims=True)
    variance = jnp.mean(center * center, axis=1, keepdims=True)
    normed = (center * lax.rsqrt(variance + 1e-05) * norm_gain + norm_bias).astype(jnp.bfloat16)
    return normed[None]


def solution(mesh):
    return jax.shard_map(
        local,
        mesh=mesh,
        in_specs=(
            P("dp", "seq", None),
            P("dp", "seq", None),
            P("dp", "seq", None),
            P(None, "seq"),
            P(),
            P("seq", "dp"),
            P(),
            P(),
            P(),
            P(),
            P(),
            P(),
        ),
        out_specs=P("dp", "seq", None),
        check_vma=False,
    )
```

profile of v0, /device:TPU:0, one launch (start us, length us, event | category | flops | bytes accessed | tf_op | source)
XLA Modules:
  0.0 230.9 jit_solution(1036459860229054314)
XLA Ops:
  7.3 50.7 %all-gather.8.cloned.1.call-done = bf16[1024,3072]{1,0:T(8,128)(2,1)} async-done(((bf16[1024,768]{1,0:T(8,128)(2,1)}), bf16[1024,3072]{1,0:T(8,128)(2,1)}) %all-gather.8.cloned.1.call-update) | async-done | bytes 6291472 | tf_op jit(solution)/shard_map/all_gather | solution.py:37
  58.0 3.8 %fusion.15 = bf16[128,3072]{1,0:T(8,128)(2,1)S(1)} fusion(bf16[1024,3072]{1,0:T(8,128)(2,1)} %all-gather.8.cloned.1.call-done, f32[3072]{0:T(1024)S(1)} %copy-done.3, bf16[1,128,1024]{2,1,0:T(8,128)(2,1)S(1)} %copy-done), kind=kOutput, calls=%fused_computation.19 | convolution fusion | flops 806092800 | bytes 7352320 | tf_op jit(solution)/shard_map/dot_general | solution.py:38
  68.4 2.6 %pad_maximum_fusion = (bf16[640,1024]{1,0:T(8,128)(2,1)S(1)}, bf16[640,1024]{1,0:T(8,128)(2,1)}) fusion(bf16[128,1024]{1,0:T(8,128)(2,1)S(1)} %copy.14, bf16[512,1024]{1,0:T(8,128)(2,1)S(1)} %bitcast.39, bf16[128,1024]{1,0:T(8,128)(2,1)S(1)} %copy.15, bf16[512,1024]{1,0:T(8,128)(2,1)} %bitcast.40), kind=kLoop, calls=%fused_computation.22 | loop fusion | flops 5242880 | bytes 5242880 | tf_op jit(solution)/shard_map/concatenate | solution.py:45
  71.0 9.1 %all-gather.10.cloned.1.call-done = bf16[512,1024]{0,1:T(8,128)(2,1)} async-done(((bf16[128,1024]{0,1:T(8,128)(2,1)}), bf16[512,1024]{0,1:T(8,128)(2,1)}) %all-gather.10.cloned.1.call-update) | async-done | bytes 1048592 | tf_op jit(solution)/shard_map/all_gather | solution.py:44
  80.1 55.4 %while.17 = (s32[]{:T(128)}, bf16[512,1024]{0,1:T(8,128)(2,1)S(1)}, f32[512,16]{0,1:T(8,128)S(1)}, f32[512,16]{0,1:T(8,128)S(1)}, bf16[512,1024]{0,1:T(8,128)(2,...) while((s32[]{:T(128)}, bf16[512,1024]{0,1:T(8,128)(2,1)S(1)}, ...), condition=%wide.region_3.4_spmd, body=%wide.region_0.3_spmd.sunk | while | flops 86900224 | bytes 5398699 | solution.py:84
  82.0 1.4 fusion.43
  85.5 1.4 fusion.43
  92.4 1.4 fusion.43
  99.3 1.4 fusion.43
  109.7 1.4 fusion.43
  113.2 1.4 fusion.43
  116.7 1.4 fusion.43
  123.6 1.4 fusion.43
  130.5 1.4 fusion.43
  134.0 1.4 fusion.43
  135.6 1.6 broadcast_in_dim.74
  138.1 28.5 %all_gather.26 = bf16[256,1024]{1,0:T(8,128)(2,1)} all-gather(bf16[256,128]{1,0:T(8,128)(2,1)S(1)} %copy-done.2), channel_id=1, replica_groups=mesh['dp'=8,'seq'=4] {'dp'}, dimensions={1}, use_global_device_ids=true | all-gather | bytes 589824 | tf_op jit(solution)/shard_map/all_gather | solution.py:103
  166.6 6.1 %all-gather = f32[2048,16]{0,1:T(8,128)S(1)} all-gather(f32[512,16]{0,1:T(8,128)S(1)} %get-tuple-element.146), channel_id=2, replica_groups=mesh['dp'=8,'seq'=4] {'seq'}, dimensions={0}, use_global_device_ids=true | all-gather | bytes 163840 | tf_op jit(solution)/shard_map/all_gather | solution.py:89
  172.8 6.2 %all-gather.1 = f32[2048,16]{0,1:T(8,128)S(1)} all-gather(f32[512,16]{0,1:T(8,128)S(1)} %get-tuple-element.147), channel_id=3, replica_groups=mesh['dp'=8,'seq'=4] {'seq'}, dimensions={0}, use_global_device_ids=true | all-gather | bytes 163840 | tf_op jit(solution)/shard_map/all_gather | solution.py:88
  179.1 17.9 %all-gather.14.cloned.1.call-done = f32[2048,1024]{0,1:T(8,128)} async-done(((f32[512,1024]{0,1:T(8,128)}), f32[2048,1024]{0,1:T(8,128)}) %all-gather.14.cloned.1.call-update) | async-done | bytes 8388624 | tf_op jit(solution)/shard_map/all_gather | solution.py:87
  197.1 10.9 %reshape.53 = f32[4,512,1024]{1,0,2:T(4,128)} reshape(f32[2048,1024]{0,1:T(8,128)} %all-gather.14.cloned.1.call-done) | data formatting | bytes 16777216 | tf_op jit(solution)/shard_map/all_gather | solution.py:87
  208.0 3.0 %fusion.16 = f32[128,1024]{0,1:T(8,128)S(1)} fusion(f32[4,512,1024]{1,0,2:T(4,128)} %reshape.53, s32[]{:T(128)S(6)} %select_n.45, f32[4,128,16]{1,0,2:T(4,128)S(1)} %get-tuple-element.179), kind=kLoop, calls=%fused_computation.21 | loop fusion | flops 917504 | bytes 2654212 | tf_op jit(solution)/shard_map/reduce_sum | solution.py:99
  211.1 10.1 %all-gather.12.cloned.1.call-done = bf16[1024,1024]{1,0:T(8,128)(2,1)} async-done(((bf16[256,1024]{1,0:T(8,128)(2,1)}), bf16[1024,1024]{1,0:T(8,128)(2,1)}) %all-gather.12.cloned.1.call-update) | async-done | bytes 2097168 | tf_op jit(solution)/shard_map/all_gather | solution.py:104
  221.1 2.1 fusion.30
  (138 shorter events, 48.3 us)
Async XLA Ops:
  6.5 51.5 %copy-start = (bf16[1,128,1024]{2,1,0:T(8,128)(2,1)S(1)}, bf16[1,128,1024]{2,1,0:T(8,128)(2,1)}, u32[]{:S(2)}) copy-start(bf16[1,128,1024]{2,1,0:T(8,128)(2,1)} %param.14) | copy-start | bytes 786436
  6.5 51.5 %copy-start.3 = (f32[3072]{0:T(1024)S(1)}, f32[3072]{0:T(1024)}, u32[]{:S(2)}) copy-start(f32[3072]{0:T(1024)} %param.18) | copy-start | bytes 36868
  6.5 51.5 %all-gather.8.cloned.1.call-start = ((), (), s32[]{:S(2)}) async-start(), calls=%async_computation | async-start | bytes 7864320 | tf_op jit(solution)/shard_map/all_gather | solution.py:37
  7.3 72.8 %all-gather.10.cloned.1.call-start = ((), (), s32[]{:S(2)}) async-start(), calls=%async_computation.1 | async-start | bytes 1310720 | tf_op jit(solution)/shard_map/all_gather | solution.py:44
  62.2 0.9 copy-start.7
  62.2 3.2 %copy-start.8 = (s32[8]{0:T(128)S(1)}, s32[8]{0:T(128)}, u32[]{:S(2)}) copy-start(s32[8]{0:T(128)} %param.24) | copy-start | bytes 100
  62.2 3.7 %copy-start.9 = (s32[8]{0:T(128)S(1)}, s32[8]{0:T(128)}, u32[]{:S(2)}) copy-start(s32[8]{0:T(128)} %param.23) | copy-start | bytes 100
  63.0 5.4 %copy-start.1 = (bf16[1,512,1024]{2,1,0:T(8,128)(2,1)S(1)}, bf16[1,512,1024]{2,1,0:T(8,128)(2,1)}, u32[]{:S(2)}) copy-start(bf16[1,512,1024]{2,1,0:T(8,128)(2,1)} %param.15) | copy-start | bytes 3145732
  63.0 134.1 %all-gather.14.cloned.1.call-start = ((), (), s32[]{:S(2)}) async-start(), calls=%async_computation.3 | async-start | bytes 10485760 | tf_op jit(solution)/shard_map/all_gather | solution.py:87
  137.2 0.8 copy-start.2
  137.2 83.9 %all-gather.12.cloned.1.call-start = ((), (), s32[]{:S(2)}) async-start(), calls=%async_computation.2 | async-start | bytes 2621440 | tf_op jit(solution)/shard_map/all_gather | solution.py:104
  208.0 13.2 %copy-start.4 = (f32[1024]{0:T(1024)S(1)}, f32[1024]{0:T(1024)}, u32[]{:S(2)}) copy-start(f32[1024]{0:T(1024)} %param.20) | copy-start | bytes 12292
  211.1 12.4 %copy-start.5 = (f32[1024]{0:T(1024)S(1)}, f32[1024]{0:T(1024)}, u32[]{:S(2)}) copy-start(f32[1024]{0:T(1024)} %param.22) | copy-start | bytes 12292
  211.1 12.4 %copy-start.6 = (f32[1024]{0:T(1024)S(1)}, f32[1024]{0:T(1024)}, u32[]{:S(2)}) copy-start(f32[1024]{0:T(1024)} %param.21) | copy-start | bytes 12292
Sparse Core Ops, SparseCore 0:
  8.9 49.0 all-gather.7
  63.1 16.8 all-gather.9
  137.4 59.6 all-gather.13
  198.5 22.5 all-gather.11
where the time goes:
time: 233 us; the launch traced here: 231 us
  waiting for transfers between devices  88.6 us (38%)
  matrix products  51.2 us (22%)
  blocking collectives  40.8 us (18%)
  local copies, waits for them, and re-layouts  17.2 us (7%)
  other arithmetic  17.2 us (7%)
  between operations  15 us (6%)
    all_gather x1, waiting for transfers between devices, local(): qkv_full = lax.all_gather(qkv_weight, 'seq', axis=1, tiled=True)  50.7 us
    all_gather x1, blocking collectives, local(): head_rows = lax.all_gather(out_weight, 'dp', axis=1, tiled=True)  28.5 us
    dot_general x16, matrix products, attend(): jnp.dot(weights.astype(jnp.bfloat16), value_block, preferred_element_type...  22.8 us
    dot_general x16, matrix products, attend(): lax.dot_general(query, key_block, (((1,), (1,)), ((), ())), preferred_ele...  22.5 us
    all_gather x1, waiting for transfers between devices, local(): lax.all_gather(partial_wide[None], 'seq', axis=0, tiled=True)  17.9 us
    all_gather x1, local copies, waits for them, and re-layouts, local(): lax.all_gather(partial_wide[None], 'seq', axis=0, tiled=True)  10.9 us
    all_gather x1, waiting for transfers between devices, local(): out_full = lax.all_gather(head_rows, 'seq', axis=0, tiled=True)  10.1 us
    all_gather x1, waiting for transfers between devices, local(): all_queries = lax.all_gather(own_queries, 'seq', axis=0, tiled=True)  9.1 us
  transfers between devices with their start and end apart: 4, of which 4 were waited for; matrix products, arithmetic and copies ran while one was open for 9% of the time, Pallas kernels for 0%

commit v1 on v0

--- a/solution.py
+++ b/solution.py
@@ -2,11 +2,27 @@
 import jax.numpy as jnp
 from jax import lax
 from jax.sharding import PartitionSpec as P
+from jax.lax import axis_index, ppermute, psum
 
 D = 1024
 HEADS = 16
 HEAD_DIM = 64
 neg_big = -1e30
+
+
+def arrange_heads_by_axis(vec, shard_axis):
+    num = psum(1, axis_name=shard_axis)
+    z2 = list(map(lambda src_i: (src_i - 1, src_i), range(1, num)))
+    seen_now = z2 + [(num - 1, 0)]
+    res = vec
+    trail = [res]
+    at = 0
+    while at < num - 1:
+        res = ppermute(res, axis_name=shard_axis, perm=seen_now)
+        trail += [res]
+        at += 1
+    front = jnp.concatenate([*reversed(trail)], 0)
+    return jnp.roll(front, shift=(axis_index(shard_axis) + 1) * res.shape[0], axis=0)
 
 
 def local(
@@ -101,7 +117,7 @@
         .astype(jnp.bfloat16)
     )
     head_rows = lax.all_gather(out_weight, "dp", axis=1, tiled=True)
-    out_full = lax.all_gather(head_rows, "seq", axis=0, tiled=True)
+    out_full = arrange_heads_by_axis(head_rows, "seq")
     projected_out = jnp.dot(attn, out_full, preferred_element_type=jnp.float32)
     mixed = projected_out + out_bias + inputs.astype(jnp.float32)
     center = mixed - jnp.mean(mixed, axis=1, keepdims=True)

time: 233 us -> 251 us (1.077)
  waiting for transfers between devices: 88.6 us -> 109 us
  blocking collectives: 40.8 us -> 38 us
    ppermute x0 -> x3, waiting for transfers between devices: none -> 48.2 us  [arrange_heads_by_axis(): res = ppermute(res, axis_name=shard_axis, perm=seen_now)]
    all_gather x1, waiting for transfers between devices: 17.9 us -> 0.02 us  [local(): lax.all_gather(partial_wide[None], 'seq', axis=0, tiled=True)]
    all_gather x1 -> x0, waiting for transfers between devices: 10.1 us -> none  [local(): out_full = lax.all_gather(head_rows, 'seq', axis=0, tiled=True)]
  transfers between devices with their start and end apart: 4 -> 6, of which waited for: 4 -> 5; matrix products, arithmetic and copies ran while one was open for 9% -> 3% of each run, Pallas kernels for 0% -> 0%
where the time goes in v1:
time: 251 us; the launch traced here: 250 us
  waiting for transfers between devices  109 us (43%)
  matrix products  51.2 us (20%)
  blocking collectives  38 us (15%)
  local copies, waits for them, and re-layouts  18.6 us (7%)
  other arithmetic  17.3 us (7%)
  between operations  15.1 us (6%)
    all_gather x1, waiting for transfers between devices, local(): qkv_full = lax.all_gather(qkv_weight, 'seq', axis=1, tiled=True)  50.7 us
    ppermute x3, waiting for transfers between devices, arrange_heads_by_axis(): res = ppermute(res, axis_name=shard_axis, perm=seen_now)  48.2 us
    all_gather x1, blocking collectives, local(): head_rows = lax.all_gather(out_weight, 'dp', axis=1, tiled=True)  27.1 us
    dot_general x16, matrix products, attend(): jnp.dot(weights.astype(jnp.bfloat16), value_block, preferred_element_type...  22.8 us
    dot_general x16, matrix products, attend(): lax.dot_general(query, key_block, (((1,), (1,)), ((), ())), preferred_ele...  22.5 us
    all_gather x1, local copies, waits for them, and re-layouts, local(): lax.all_gather(partial_wide[None], 'seq', axis=0, tiled=True)  10.8 us
    all_gather x1, waiting for transfers between devices, local(): all_queries = lax.all_gather(own_queries, 'seq', axis=0, tiled=True)  9.1 us
    reduce_sum x16, other arithmetic, attend(): total = jnp.sum(weights, axis=1)  7.31 us
  transfers between devices with their start and end apart: 6, of which 5 were waited for; matrix products, arithmetic and copies ran while one was open for 3% of the time, Pallas kernels for 0%

profile of v1, /device:TPU:0, one launch (start us, length us, event | category | flops | bytes accessed | tf_op | source)
XLA Modules:
  0.0 249.8 jit_solution(15147377718544319950)
XLA Ops:
  7.3 50.7 %all-gather.7.cloned.1.call-done = bf16[1024,3072]{1,0:T(8,128)(2,1)} async-done(((bf16[1024,768]{1,0:T(8,128)(2,1)}), bf16[1024,3072]{1,0:T(8,128)(2,1)}) %all-gather.7.cloned.1.call-update) | async-done | bytes 6291472 | tf_op jit(solution)/shard_map/all_gather | solution.py:53
  58.0 3.8 %fusion.15 = bf16[128,3072]{1,0:T(8,128)(2,1)S(1)} fusion(bf16[1024,3072]{1,0:T(8,128)(2,1)} %all-gather.7.cloned.1.call-done, f32[3072]{0:T(1024)} %param.18, bf16[1,128,1024]{2,1,0:T(8,128)(2,1)} %param.14), kind=kOutput, calls=%fused_computation.19 | convolution fusion | flops 806092800 | bytes 7352320 | tf_op jit(solution)/shard_map/dot_general | solution.py:54
  68.4 2.6 %pad_maximum_fusion = (bf16[640,1024]{1,0:T(8,128)(2,1)S(1)}, bf16[640,1024]{1,0:T(8,128)(2,1)}) fusion(bf16[128,1024]{1,0:T(8,128)(2,1)S(1)} %copy.14, bf16[512,1024]{1,0:T(8,128)(2,1)S(1)} %bitcast.38, bf16[128,1024]{1,0:T(8,128)(2,1)S(1)} %copy.15, bf16[512,1024]{1,0:T(8,128)(2,1)} %bitcast.39), kind=kLoop, calls=%fused_computation.24 | loop fusion | flops 5242880 | bytes 5242880 | tf_op jit(solution)/shard_map/concatenate | solution.py:61
  71.0 9.1 %all-gather.9.cloned.1.call-done = bf16[512,1024]{0,1:T(8,128)(2,1)} async-done(((bf16[128,1024]{0,1:T(8,128)(2,1)}), bf16[512,1024]{0,1:T(8,128)(2,1)}) %all-gather.9.cloned.1.call-update) | async-done | bytes 1048592 | tf_op jit(solution)/shard_map/all_gather | solution.py:60
  80.1 55.4 %while.17 = (s32[]{:T(128)}, bf16[512,1024]{0,1:T(8,128)(2,1)S(1)}, f32[512,16]{0,1:T(8,128)S(1)}, f32[512,16]{0,1:T(8,128)S(1)}, bf16[512,1024]{0,1:T(8,128)(2,...) while((s32[]{:T(128)}, bf16[512,1024]{0,1:T(8,128)(2,1)S(1)}, ...), condition=%wide.region_3.4_spmd, body=%wide.region_0.3_spmd.sunk | while | flops 86900224 | bytes 5398699 | solution.py:100
  82.0 1.4 fusion.50
  89.0 1.4 fusion.50
  95.9 1.4 fusion.50
  102.8 1.4 fusion.50
  106.3 1.4 fusion.50
  113.2 1.4 fusion.50
  120.1 1.4 fusion.50
  127.1 1.4 fusion.50
  135.6 1.6 broadcast_in_dim.74
  137.3 27.1 %all_gather.23 = bf16[256,1024]{1,0:T(8,128)(2,1)S(1)} all-gather(bf16[256,128]{1,0:T(8,128)(2,1)S(1)} %copy-done.3), channel_id=1, replica_groups=mesh['dp'=8,'seq'=4] {'dp'}, dimensions={1}, use_global_device_ids=true | all-gather | bytes 589824 | tf_op jit(solution)/shard_map/all_gather | solution.py:119
  164.4 19.8 %collective-permute-done = bf16[256,1024]{1,0:T(8,128)(2,1)S(1)} collective-permute-done((bf16[256,1024]{1,0:T(8,128)(2,1)S(1)}, bf16[256,1024]{1,0:T(8,128)(2,1)S(1)}, u32[]{:S(2)}, u32[]{:S(2)}) %collective-permute-start) | collective-permute-done | bytes 524320 | tf_op jit(solution)/shard_map/ppermute | solution.py:21
  184.2 19.8 %collective-permute-done.1 = bf16[256,1024]{1,0:T(8,128)(2,1)S(1)} collective-permute-done((bf16[256,1024]{1,0:T(8,128)(2,1)S(1)}, bf16[256,1024]{1,0:T(8,128)(2,1)S(1)}, u32[]{:S(2)}, u32[]{:S(2)}) %collective-permute-start.1) | collective-permute-done | bytes 524320 | tf_op jit(solution)/shard_map/ppermute | solution.py:21
  204.0 8.6 %collective-permute-done.2 = bf16[256,1024]{1,0:T(8,128)(2,1)S(1)} collective-permute-done((bf16[256,1024]{1,0:T(8,128)(2,1)S(1)}, bf16[256,1024]{1,0:T(8,128)(2,1)S(1)}, u32[]{:S(2)}, u32[]{:S(2)}) %collective-permute-start.2) | collective-permute-done | bytes 524320 | tf_op jit(solution)/shard_map/ppermute | solution.py:21
  213.0 1.9 copy-done.1
  214.9 5.4 %all-gather = f32[2048,16]{0,1:T(8,128)S(1)} all-gather(f32[512,16]{0,1:T(8,128)S(1)} %get-tuple-element.146), channel_id=2, replica_groups=mesh['dp'=8,'seq'=4] {'seq'}, dimensions={0}, use_global_device_ids=true | all-gather | bytes 163840 | tf_op jit(solution)/shard_map/all_gather | solution.py:105
  220.4 5.4 %all-gather.1 = f32[2048,16]{0,1:T(8,128)S(1)} all-gather(f32[512,16]{0,1:T(8,128)S(1)} %get-tuple-element.147), channel_id=3, replica_groups=mesh['dp'=8,'seq'=4] {'seq'}, dimensions={0}, use_global_device_ids=true | all-gather | bytes 163840 | tf_op jit(solution)/shard_map/all_gather | solution.py:104
  226.0 10.8 %reshape.53 = f32[4,512,1024]{1,0,2:T(4,128)} reshape(f32[2048,1024]{0,1:T(8,128)} %all-gather.11.cloned.1.call-done) | data formatting | bytes 16777216 | tf_op jit(solution)/shard_map/all_gather | solution.py:103
  236.8 3.1 %fusion.16 = f32[128,1024]{0,1:T(8,128)S(1)} fusion(f32[4,512,1024]{1,0,2:T(4,128)} %reshape.53, s32[]{:T(128)S(6)} %select_n.58, f32[4,128,16]{1,0,2:T(4,128)S(1)} %get-tuple-element.179), kind=kLoop, calls=%fused_computation.21 | loop fusion | flops 917504 | bytes 2654212 | tf_op jit(solution)/shard_map/reduce_sum | solution.py:115
  240.0 2.1 fusion.38
  (149 shorter events, 50.6 us)
Async XLA Ops:
  6.5 51.5 %all-gather.7.cloned.1.call-start = ((), (), s32[]{:S(2)}) async-start(), calls=%async_computation | async-start | bytes 7864320 | tf_op jit(solution)/shard_map/all_gather | solution.py:53
  7.3 72.8 %all-gather.9.cloned.1.call-start = ((), (), s32[]{:S(2)}) async-start(), calls=%async_computation.1 | async-start | bytes 1310720 | tf_op jit(solution)/shard_map/all_gather | solution.py:60
  61.8 1.3 copy-start.7
  61.8 3.6 %copy-start.8 = (s32[8]{0:T(128)S(1)}, s32[8]{0:T(128)}, u32[]{:S(2)}) copy-start(s32[8]{0:T(128)} %param.24) | copy-start | bytes 100
  61.8 4.1 %copy-start.9 = (s32[8]{0:T(128)S(1)}, s32[8]{0:T(128)}, u32[]{:S(2)}) copy-start(s32[8]{0:T(128)} %param.23) | copy-start | bytes 100
  62.2 6.2 %copy-start.2 = (bf16[1,512,1024]{2,1,0:T(8,128)(2,1)S(1)}, bf16[1,512,1024]{2,1,0:T(8,128)(2,1)}, u32[]{:S(2)}) copy-start(bf16[1,512,1024]{2,1,0:T(8,128)(2,1)} %param.15) | copy-start | bytes 3145732
  63.0 163.0 %all-gather.11.cloned.1.call-start = ((), (), s32[]{:S(2)}) async-start(), calls=%async_computation.2 | async-start | bytes 10485760 | tf_op jit(solution)/shard_map/all_gather | solution.py:103
  135.6 1.7 copy-start.3
  164.4 19.8 %collective-permute-start = (bf16[256,1024]{1,0:T(8,128)(2,1)S(1)}, bf16[256,1024]{1,0:T(8,128)(2,1)S(1)}, u32[]{:S(2)}, u32[]{:S(2)}) collective-permute-start(bf16[256,1024]{1,0:T(8,128)(2,1)S(1)} %all_gather.23), channel_id=1, source_target_pairs={{0,1},{1,2},{2,3},{3,0},{4,5},{5,6},{6,7},{7,4},{8,9},{9,10},{10,1... | collective-permute-start | bytes 1572872 | tf_op jit(solution)/shard_map/ppermute | solution.py:21
  184.2 19.8 %collective-permute-start.1 = (bf16[256,1024]{1,0:T(8,128)(2,1)S(1)}, bf16[256,1024]{1,0:T(8,128)(2,1)S(1)}, u32[]{:S(2)}, u32[]{:S(2)}) collective-permute-start(bf16[256,1024]{1,0:T(8,128)(2,1)S(1)} %collective-permute-done), channel_id=1, source_target_pairs={{0,1},{1,2},{2,3},{3,0},{4,5},{5,6},{6,7},{7,4},{8,9},{9,10},{10,1... | collective-permute-start | bytes 1572872 | tf_op jit(solution)/shard_map/ppermute | solution.py:21
  204.0 8.6 %collective-permute-start.2 = (bf16[256,1024]{1,0:T(8,128)(2,1)S(1)}, bf16[256,1024]{1,0:T(8,128)(2,1)S(1)}, u32[]{:S(2)}, u32[]{:S(2)}) collective-permute-start(bf16[256,1024]{1,0:T(8,128)(2,1)S(1)} %collective-permute-done.1), channel_id=1, source_target_pairs={{0,1},{1,2},{2,3},{3,0},{4,5},{5,6},{6,7},{7,4},{8,9},{9,10},{10,1... | collective-permute-start | bytes 1572872 | tf_op jit(solution)/shard_map/ppermute | solution.py:21
  213.0 1.9 copy-start.1
  236.8 3.1 %copy-start = (bf16[1,128,1024]{2,1,0:T(8,128)(2,1)S(1)}, bf16[1,128,1024]{2,1,0:T(8,128)(2,1)}, u32[]{:S(2)}) copy-start(bf16[1,128,1024]{2,1,0:T(8,128)(2,1)} %param.14) | copy-start | bytes 786436
  236.8 3.2 %copy-start.4 = (f32[1024]{0:T(1024)S(1)}, f32[1024]{0:T(1024)}, u32[]{:S(2)}) copy-start(f32[1024]{0:T(1024)} %param.20) | copy-start | bytes 12292
  239.9 2.5 copy-start.5
  239.9 2.5 copy-start.6
Sparse Core Ops, SparseCore 0:
  8.9 49.0 all-gather.6
  63.1 16.8 all-gather.8
  137.4 69.5 all-gather.10
